TPU v7x, 256 devices: a whole 4x4x8 slice. The times are simulated.
256 devices in a mesh: seq: 16 (over y, x_lo, core), fsdp: 16 (over z, x_hi).
Axes of the slice: x: 4 (x_hi: 2, x_lo: 2; x = x_hi * 2 + x_lo), y: 4, z: 8, core: 2. Of those that a mesh axis runs over, the one named last changes fastest.
Arguments:
- clean_states: bfloat16 [16, 4096, 4096], P('fsdp', 'seq'), may hold values from -6 to 6
- noise_mask: int32 [16, 4096], P('fsdp', 'seq'), may hold values from 0 to 1, as said below
- mask_embed: bfloat16 [4096], replicated, may hold values from -6 to 6
- queries: bfloat16 [16, 4096, 2048], P('fsdp', 'seq'), may hold values from -96 to 96
- w_key: bfloat16 [4096, 512], P('fsdp'), may hold values from -0.09375 to 0.09375
- w_value: bfloat16 [4096, 512], P('fsdp'), may hold values from -0.09375 to 0.09375
Outputs:
- noisy_attention: bfloat16 [16, 4096, 2048], P('fsdp', 'seq')
Inputs may be any that keep to these rules, and one draw needn't show every extreme that they name: `noise_mask`: each block of 256 positions has its own masking rate; 1 marks a masked position.
All inputs are finite; a program needn't handle non-finite values.
Results may differ from a plain program's by a relative error of at most 0.011.
Values may be sent and summed in bfloat16 or wider, within the bound.
A program may use at most 64 MiB of HBM per device.

v0:
```python
import jax
import jax.numpy as jnp
from jax import lax
from jax.sharding import PartitionSpec as P

HEADS = 16
HEAD_DIM = 128
BLOCK = 256
ROPE_BASE = 500000.0


def rotate(key_rows, positions):
    half_dim = key_rows.shape[-1] // 2
    frequency = ROPE_BASE ** (-(jnp.arange(half_dim, dtype=jnp.float32) * 2.0 / key_rows.shape[-1]))
    angles = positions[:, None] * frequency[None, :]
    cosine = jnp.cos(angles)[:, None, :]
    sine_part = jnp.sin(angles)[:, None, :]
    first_half = key_rows[..., :half_dim]
    second_half = key_rows[..., half_dim:]
    return jnp.concatenate(
        [
            first_half * cosine - second_half * sine_part,
            second_half * cosine + first_half * sine_part,
        ],
        -1,
    )


def shards(clean_states, noise_mask, mask_embed, queries, w_key, w_value):
    states = clean_states[0]
    noise_marks = noise_mask[0]
    length_dev = states.shape[0]
    kv_width = w_key.shape[1]
    kv_count = kv_width // HEAD_DIM
    groups = HEADS // kv_count
    score_scale = HEAD_DIM ** (-0.5)
    query_rows = queries[0].reshape(length_dev, kv_count, groups, HEAD_DIM)
    source_rows = jnp.concatenate([states, mask_embed[None, :]], 0)
    pieces = (
        lax.all_gather(w_key, "fsdp", axis=0, tiled=True),
        lax.all_gather(w_value, "fsdp", axis=0, tiled=True),
    )
    key_all = jnp.dot(source_rows, pieces[0], preferred_element_type=jnp.float32)
    value_all = jnp.dot(source_rows, pieces[1], preferred_element_type=jnp.float32)
    masked_rows = noise_marks[:, None] == 1
    clean_key_sums = key_all[:length_dev]
    clean_value_sums = value_all[:length_dev]
    noisy_key_sums = jnp.where(masked_rows, key_all[length_dev:], clean_key_sums)
    noisy_value_sums = jnp.where(masked_rows, value_all[length_dev:], clean_value_sums)
    key_sums = jnp.concatenate([clean_key_sums, noisy_key_sums], 0)
    value_sums = jnp.concatenate([clean_value_sums, noisy_value_sums], 0)
    first_row = lax.axis_index("seq") * length_dev
    positions = first_row + jnp.arange(length_dev, dtype=jnp.int32)
    both_positions = jnp.concatenate([positions, positions]).astype(jnp.float32)
    key_rows = (
        rotate(key_sums.reshape(2 * length_dev, kv_count, HEAD_DIM), both_positions)
        .astype(jnp.bfloat16)
        .reshape(2 * length_dev, kv_width)
    )
    value_rows = value_sums.astype(jnp.bfloat16)
    clean_keys = key_rows[:length_dev]
    clean_values = value_rows[:length_dev]
    noisy_keys = key_rows[length_dev:]
    noisy_values = value_rows[length_dev:]
    query_block = positions // BLOCK

    def absorb(running, key_part, value_part, allowed):
        row_max, row_sum, mixture = running
        key_count = key_part.shape[0]
        scores = (
            jnp.einsum(
                "qkgd,tkd->qkgt",
                query_rows,
                key_part.reshape(key_count, kv_count, HEAD_DIM),
                preferred_element_type=jnp.float32,
            )
            * score_scale
        )
        mask_wide = allowed[:, None, None, :]
        scores = jnp.where(mask_wide, scores, -1e30)
        new_max = jnp.maximum(row_max, jnp.max(scores, -1))
        weights = jnp.where(mask_wide, jnp.exp(scores - new_max[..., None]), 0.0)
        rescale = jnp.exp(row_max - new_max)
        row_sum = row_sum * rescale + jnp.sum(weights, -1)
        mixture = mixture * rescale[..., None] + jnp.einsum(
            "qkgt,tkd->qkgd",
            weights.astype(jnp.bfloat16),
            value_part.reshape(key_count, kv_count, HEAD_DIM),
            preferred_element_type=jnp.float32,
        )
        return (new_max, row_sum, mixture)

    def sweep(running, key_stack, value_stack, start_row, same_copy):
        rounds = key_stack.shape[0] // BLOCK

        def sub_step(number, running):
            offset = number * BLOCK
            key_part = lax.dynamic_slice_in_dim(key_stack, offset, BLOCK, 0)
            value_part = lax.dynamic_slice_in_dim(value_stack, offset, BLOCK, 0)
            key_block = (start_row + offset) // BLOCK
            if same_copy:
                allowed = query_block[:, None] == key_block
            else:
                allowed = (query_block[:, None] > key_block) & (key_block >= 0)
            allowed = jnp.broadcast_to(allowed, (length_dev, BLOCK))
            return absorb(running, key_part, value_part, allowed)

        return lax.fori_loop(0, rounds, sub_step, running)

    running = (
        jnp.full((length_dev, kv_count, groups), -1e30, jnp.float32),
        jnp.zeros((length_dev, kv_count, groups), jnp.float32),
        jnp.zeros((length_dev, kv_count, groups, HEAD_DIM), jnp.float32),
    )
    running = sweep(running, noisy_keys, noisy_values, first_row, True)
    pieces = (
        lax.all_gather(clean_keys, "seq", axis=0, tiled=True),
        lax.all_gather(clean_values, "seq", axis=0, tiled=True),
    )
    running = sweep(running, pieces[0], pieces[1], jnp.int32(0), False)
    row_max, row_sum, mixture = running
    output = (
        (mixture / row_sum[..., None])
        .astype(jnp.bfloat16)
        .reshape(length_dev, kv_count * groups * HEAD_DIM)
    )
    return output[None]


def solution(mesh):
    placed = (
        P("fsdp", "seq", None),
        P("fsdp", "seq"),
        P(),
        P("fsdp", "seq", None),
        P("fsdp", None),
        P("fsdp", None),
    )
    return jax.shard_map(
        shards, mesh=mesh, in_specs=placed, out_specs=P("fsdp", "seq", None), check_vma=False
    )
```

profile of v0, /device:TPU:1, one launch (start us, length us, event | category | flops | bytes accessed | tf_op | source)
XLA Modules:
  0.0 420.3 jit_solution(12876547095858596038)
XLA Ops:
  9.5 101.1 %all-gather.7.cloned.1.call-done = bf16[4096,512]{1,0:T(8,128)(2,1)} async-done(((bf16[256,512]{1,0:T(8,128)(2,1)}), bf16[4096,512]{1,0:T(8,128)(2,1)}) %all-gather.7.cloned.1.call-update) | async-done | bytes 4194320 | tf_op jit(solution)/shard_map/all_gather | solution.py:41
  110.5 4.2 %fusion.33 = f32[257,512]{1,0:T(8,128)S(1)} fusion(bf16[4096,512]{1,0:T(8,128)(2,1)} %all-gather.7.cloned.1.call-done, bf16[1,4096]{1,0:T(2,128)(2,1)S(1)} %broadcast_in_dim.141, bf16[256,4096]{1,0:T(8,128)(2,1)} %bitcast.118), kind=kOutput, calls=%fused_computation.45 | convolution fusion | flops 1082146816 | bytes 6825984 | tf_op jit(solution)/shard_map/dot_general | solution.py:44
  115.7 1.0 multiply_cosine_fusion
  116.7 93.1 %all-gather.5.cloned.1.call-done = bf16[4096,512]{1,0:T(8,128)(2,1)} async-done(((bf16[256,512]{1,0:T(8,128)(2,1)}), bf16[4096,512]{1,0:T(8,128)(2,1)}) %all-gather.5.cloned.1.call-update) | async-done | bytes 4194320 | tf_op jit(solution)/shard_map/all_gather | solution.py:40
  209.7 3.5 fusion.34
  215.7 1.5 copy.18
  219.7 1.0 fusion.22
  220.8 2.5 bitcast_add_fusion.1
  223.3 28.4 %all-gather.11.cloned.1.call-done = bf16[4096,512]{1,0:T(8,128)(2,1)} async-done(((bf16[256,512]{1,0:T(8,128)(2,1)}), bf16[4096,512]{1,0:T(8,128)(2,1)}) %all-gather.11.cloned.1.call-update) | async-done | bytes 4194320 | tf_op jit(solution)/shard_map/all_gather | solution.py:118
  251.7 50.2 %all-gather.9.cloned.1.call-done = bf16[4096,512]{0,1:T(8,128)(2,1)} async-done(((bf16[256,512]{0,1:T(8,128)(2,1)}), bf16[4096,512]{0,1:T(8,128)(2,1)}) %all-gather.9.cloned.1.call-update) | async-done | bytes 4194320 | tf_op jit(solution)/shard_map/all_gather | solution.py:117
  301.9 108.7 %while.13 = (s32[]{:T(128)}, f32[256,4,4]{0,2,1:T(4,128)S(1)}, f32[256,4,4]{0,2,1:T(4,128)S(1)}, f32[256,4,4,128]{0,3,2,1:T(8,128)}, bf16[4096,512]{0,1:T(8,128)...) while((s32[]{:T(128)}, f32[256,4,4]{0,2,1:T(4,128)S(1)}, ...), condition=%wide.region_5.6_spmd.clone, body=%wide.region_2.5_spmd.clone.sunk | while | flops 551563776 | bytes 36963736 | solution.py:108
  303.0 1.0 constant_dynamic-slice_fusion.4
  304.9 1.0 fusion.66
  305.9 1.4 bitcast_add_fusion.3
  307.3 1.4 copy-done.1
  309.8 1.0 constant_dynamic-slice_fusion.4
  311.7 1.0 fusion.66
  312.7 1.4 bitcast_add_fusion.3
  314.1 1.4 copy-done.1
  316.6 1.0 constant_dynamic-slice_fusion.4
  318.4 1.0 fusion.66
  319.5 1.4 bitcast_add_fusion.3
  320.9 1.4 copy-done.1
  325.2 1.0 fusion.66
  326.3 1.4 bitcast_add_fusion.3
  327.7 1.4 copy-done.1
  332.0 1.0 fusion.66
  333.1 1.4 bitcast_add_fusion.3
  334.5 1.4 copy-done.1
  338.8 1.0 fusion.66
  339.9 1.4 bitcast_add_fusion.3
  341.3 1.4 copy-done.1
  345.6 1.0 fusion.66
  346.7 1.4 bitcast_add_fusion.3
  348.1 1.4 copy-done.1
  352.4 1.0 fusion.66
  353.5 1.4 bitcast_add_fusion.3
  354.9 1.4 copy-done.1
  359.2 1.0 fusion.66
  360.3 1.4 bitcast_add_fusion.3
  361.7 1.4 copy-done.1
  366.0 1.0 fusion.66
  367.1 1.4 bitcast_add_fusion.3
  368.5 1.4 copy-done.1
  372.8 1.0 fusion.66
  373.8 1.4 bitcast_add_fusion.3
  375.3 1.4 copy-done.1
  379.6 1.0 fusion.66
  380.6 1.4 bitcast_add_fusion.3
  382.1 1.4 copy-done.1
  386.4 1.0 fusion.66
  387.4 1.4 bitcast_add_fusion.3
  388.9 1.4 copy-done.1
  393.2 1.0 fusion.66
  394.2 1.4 bitcast_add_fusion.3
  395.6 1.4 copy-done.1
  400.0 1.0 fusion.66
  401.0 1.4 bitcast_add_fusion.3
  402.4 1.4 copy-done.1
  406.8 1.0 fusion.66
  407.8 1.4 bitcast_add_fusion.3
  409.2 1.4 copy-done.1
  410.6 1.8 divide_convert_fusion
  412.4 1.4 copy.34
  (206 shorter events, 53.0 us)
Async XLA Ops:
  6.5 104.0 %all-gather.7.cloned.1.call-start = ((), (), s32[]{:S(2)}) async-start(), calls=%async_computation.1 | async-start | bytes 4456448 | tf_op jit(solution)/shard_map/all_gather | solution.py:41
  7.3 202.5 %all-gather.5.cloned.1.call-start = ((), (), s32[]{:S(2)}) async-start(), calls=%async_computation | async-start | bytes 4456448 | tf_op jit(solution)/shard_map/all_gather | solution.py:40
  8.0 243.7 %all-gather.11.cloned.1.call-start = ((), (), s32[]{:S(2)}) async-start(), calls=%async_computation.3 | async-start | bytes 4456448 | tf_op jit(solution)/shard_map/all_gather | solution.py:118
  110.5 99.2 %copy-start.3 = (bf16[1,256,4096]{2,1,0:T(8,128)(2,1)S(1)}, bf16[1,256,4096]{2,1,0:T(8,128)(2,1)}, u32[]{:S(2)}) copy-start(bf16[1,256,4096]{2,1,0:T(8,128)(2,1)} %param.8) | copy-start | bytes 6291460
  115.6 186.3 %all-gather.9.cloned.1.call-start = ((), (), s32[]{:S(2)}) async-start(), calls=%async_computation.2 | async-start | bytes 4456448 | tf_op jit(solution)/shard_map/all_gather | solution.py:117
  218.8 1.9 copy-start.2
  304.0 1.9 copy-start
  307.3 1.4 copy-start.1
  310.8 1.9 copy-start
  314.1 1.4 copy-start.1
  317.6 1.9 copy-start
  320.9 1.4 copy-start.1
  324.4 1.9 copy-start
  327.7 1.4 copy-start.1
  331.2 1.9 copy-start
  334.5 1.4 copy-start.1
  338.0 1.9 copy-start
  341.3 1.4 copy-start.1
  344.8 1.9 copy-start
  348.1 1.4 copy-start.1
  351.6 1.9 copy-start
  354.9 1.4 copy-start.1
  358.3 1.9 copy-start
  361.7 1.4 copy-start.1
  365.1 1.9 copy-start
  368.4 1.4 copy-start.1
  371.9 1.9 copy-start
  375.2 1.4 copy-start.1
  378.7 1.9 copy-start
  382.0 1.4 copy-start.1
  385.5 1.9 copy-start
  388.8 1.4 copy-start.1
  392.3 1.9 copy-start
  395.6 1.4 copy-start.1
  399.1 1.9 copy-start
  402.4 1.4 copy-start.1
  405.9 1.9 copy-start
  409.2 1.4 copy-start.1
Sparse Core Ops, SparseCore 0:
  9.9 100.5 all-gather.6
  113.1 96.5 all-gather.4
  211.6 40.0 all-gather.10
  253.3 48.5 all-gather.8
where the time goes:
time: 422 us; the launch traced here: 420 us
  waiting for transfers between devices  274 us (65%)
  local copies, waits for them, and re-layouts  62 us (15%)
  matrix products  46.7 us (11%)
  other arithmetic  22.8 us (5%)
  between operations  13.3 us (3%)
    all_gather x1, waiting for transfers between devices, shards(): lax.all_gather(w_value, 'fsdp', axis=0, tiled=True)  101 us
    all_gather x1, waiting for transfers between devices, shards(): lax.all_gather(w_key, 'fsdp', axis=0, tiled=True)  93.1 us
    all_gather x1, waiting for transfers between devices, shards(): lax.all_gather(clean_keys, 'seq', axis=0, tiled=True)  50.2 us
    all_gather x1, waiting for transfers between devices, shards(): lax.all_gather(clean_values, 'seq', axis=0, tiled=True)  28.4 us
    dot_general x17, matrix products, absorb(): jnp.einsum('qkgt,tkd->qkgd', weights.astype(jnp.bfloat16), value_part.res...  24.7 us
    while x80, local copies, waits for them, and re-layouts  21.8 us
    dynamic_slice x32, local copies, waits for them, and re-layouts, sub_step(): value_part = lax.dynamic_slice_in_dim(value_stack, offset, BLOCK, 0)  17.7 us
    reduce_sum x17, other arithmetic, absorb(): row_sum = row_sum * rescale + jnp.sum(weights, -1)  17.4 us
  transfers between devices with their start and end apart: 4, of which 4 were waited for; matrix products, arithmetic and copies ran while one was open for 5% of the time, Pallas kernels for 0%

commit v1 on v0

--- a/solution.py
+++ b/solution.py
@@ -38,7 +38,9 @@
     source_rows = jnp.concatenate([states, mask_embed[None, :]], 0)
     pieces = (
         lax.all_gather(w_key, "fsdp", axis=0, tiled=True),
-        lax.all_gather(w_value, "fsdp", axis=0, tiled=True),
+        jnp.concatenate(
+            lax.all_to_all(jnp.stack([w_value] * lax.axis_size("fsdp")), "fsdp", 0, 0), axis=0
+        ),
     )
     key_all = jnp.dot(source_rows, pieces[0], preferred_element_type=jnp.float32)
     value_all = jnp.dot(source_rows, pieces[1], preferred_element_type=jnp.float32)

time: 422 us -> 382 us (0.905)
  waiting for transfers between devices: 274 us -> 221 us
  starting transfers between devices: 0.12 us -> 12 us
    all_gather x1 -> x0, waiting for transfers between devices: 101 us -> none  [shards(): lax.all_gather(w_value, 'fsdp', axis=0, tiled=True)]
    all_gather x1, waiting for transfers between devices: 93.1 us -> 143 us  [shards(): lax.all_gather(w_key, 'fsdp', axis=0, tiled=True)]
    all_gather x1, waiting for transfers between devices: 50.2 us -> 36.6 us  [shards(): lax.all_gather(clean_keys, 'seq', axis=0, tiled=True)]
    all_gather x1, waiting for transfers between devices: 28.4 us -> 41.1 us  [shards(): lax.all_gather(clean_values, 'seq', axis=0, tiled=True)]
    all_to_all x0 -> x1, starting transfers between devices: none -> 11.8 us  [shards(): lax.all_to_all(jnp.stack([w_value] * lax.axis_size('fsdp')), 'fsdp', 0, 0)]
  transfers between devices with their start and end apart: 4 -> 4, of which waited for: 4 -> 3; matrix products, arithmetic and copies ran while one was open for 5% -> 6% of each run, Pallas kernels for 0% -> 0%
where the time goes in v1:
time: 382 us; the launch traced here: 381 us
  waiting for transfers between devices  221 us (58%)
  local copies, waits for them, and re-layouts  63.7 us (17%)
  matrix products  47.1 us (12%)
  other arithmetic  22.2 us (6%)
  between operations  13.3 us (3%)
  starting transfers between devices  12 us (3%)
    all_gather x1, waiting for transfers between devices, shards(): lax.all_gather(w_key, 'fsdp', axis=0, tiled=True)  143 us
    all_gather x1, waiting for transfers between devices, shards(): lax.all_gather(clean_values, 'seq', axis=0, tiled=True)  41.1 us
    all_gather x1, waiting for transfers between devices, shards(): lax.all_gather(clean_keys, 'seq', axis=0, tiled=True)  36.6 us
    dot_general x17, matrix products, absorb(): jnp.einsum('qkgt,tkd->qkgd', weights.astype(jnp.bfloat16), value_part.res...  24.7 us
    while x80, local copies, waits for them, and re-layouts  21.7 us
    dynamic_slice x32, local copies, waits for them, and re-layouts, sub_step(): value_part = lax.dynamic_slice_in_dim(value_stack, offset, BLOCK, 0)  17.7 us
    reduce_sum x17, other arithmetic, absorb(): row_sum = row_sum * rescale + jnp.sum(weights, -1)  17.4 us
    dynamic_slice x16, local copies, waits for them, and re-layouts, sub_step(): key_part = lax.dynamic_slice_in_dim(key_stack, offset, BLOCK, 0)  15.6 us
  transfers between devices with their start and end apart: 4, of which 3 were waited for; matrix products, arithmetic and copies ran while one was open for 6% of the time, Pallas kernels for 0%

profile of v1, /device:TPU:1, one launch (start us, length us, event | category | flops | bytes accessed | tf_op | source)
XLA Modules:
  0.0 380.8 jit_solution(10466287877192879846)
XLA Ops:
  7.3 3.3 stack.2
  10.6 11.8 %all-to-all-start = ((bf16[16,256,512]{2,1,0:T(8,128)(2,1)}), bf16[16,256,512]{2,1,0:T(8,128)(2,1)}, u32[]{:S(2)}, u32[]{:S(2)}) async-start(bf16[16,256,512]{2,1,0:T(8,128)(2,1)} %stack.2), calls=%async_computation | async-start | bytes 8388608 | tf_op jit(solution)/shard_map/all_to_all | solution.py:42
  22.5 1.0 multiply_cosine_fusion
  23.5 142.8 %all-gather.4.cloned.1.call-done = bf16[4096,512]{1,0:T(8,128)(2,1)} async-done(((bf16[256,512]{1,0:T(8,128)(2,1)}), bf16[4096,512]{1,0:T(8,128)(2,1)}) %all-gather.4.cloned.1.call-update) | async-done | bytes 4194320 | tf_op jit(solution)/shard_map/all_gather | solution.py:40
  166.3 4.1 %fusion.34 = f32[257,512]{1,0:T(8,128)S(1)} fusion(bf16[4096,512]{1,0:T(8,128)(2,1)} %all-gather.4.cloned.1.call-done, bf16[1,4096]{1,0:T(2,128)(2,1)S(1)} %broadcast_in_dim.141, bf16[256,4096]{1,0:T(8,128)(2,1)} %bitcast.119), kind=kOutput, calls=%fused_computation.46 | convolution fusion | flops 1082146816 | bytes 6825984 | tf_op jit(solution)/shard_map/dot_general | solution.py:45
  173.1 4.2 %fusion.33 = f32[257,512]{1,0:T(8,128)S(1)} fusion(bf16[4096,512]{1,0:T(8,128)(2,1)} %bitcast.6, bf16[1,4096]{1,0:T(2,128)(2,1)S(1)} %broadcast_in_dim.141, bf16[256,4096]{1,0:T(8,128)(2,1)} %bitcast.120), kind=kOutput, calls=%fused_computation.45 | convolution fusion | flops 1082146816 | bytes 6825984 | tf_op jit(solution)/shard_map/dot_general | solution.py:46
  181.1 1.0 fusion.22
  182.2 2.5 bitcast_add_fusion.1
  184.7 36.6 %all-gather.6.cloned.1.call-done = bf16[4096,512]{0,1:T(8,128)(2,1)} async-done(((bf16[256,512]{0,1:T(8,128)(2,1)}), bf16[4096,512]{0,1:T(8,128)(2,1)}) %all-gather.6.cloned.1.call-update) | async-done | bytes 4194320 | tf_op jit(solution)/shard_map/all_gather | solution.py:119
  221.3 41.1 %all-gather.8.cloned.1.call-done = bf16[4096,512]{1,0:T(8,128)(2,1)} async-done(((bf16[256,512]{1,0:T(8,128)(2,1)}), bf16[4096,512]{1,0:T(8,128)(2,1)}) %all-gather.8.cloned.1.call-update) | async-done | bytes 4194320 | tf_op jit(solution)/shard_map/all_gather | solution.py:120
  262.4 108.6 %while.13 = (s32[]{:T(128)}, f32[256,4,4]{0,2,1:T(4,128)S(1)}, f32[256,4,4]{0,2,1:T(4,128)S(1)}, f32[256,4,4,128]{0,3,2,1:T(8,128)}, bf16[4096,512]{0,1:T(8,128)...) while((s32[]{:T(128)}, f32[256,4,4]{0,2,1:T(4,128)S(1)}, ...), condition=%wide.region_5.6_spmd.clone, body=%wide.region_2.5_spmd.clone.sunk | while | flops 551563776 | bytes 36963736 | solution.py:110
  265.4 1.0 fusion.66
  266.5 1.4 bitcast_add_fusion.3
  267.9 1.3 copy-done.1
  272.2 1.0 fusion.66
  273.2 1.4 bitcast_add_fusion.3
  274.7 1.3 copy-done.1
  277.1 1.0 constant_dynamic-slice_fusion.4
  279.0 1.0 fusion.66
  280.0 1.4 bitcast_add_fusion.3
  281.4 1.3 copy-done.1
  285.8 1.0 fusion.66
  286.8 1.4 bitcast_add_fusion.3
  288.2 1.3 copy-done.1
  292.6 1.0 fusion.66
  293.6 1.4 bitcast_add_fusion.3
  295.0 1.3 copy-done.1
  299.3 1.0 fusion.66
  300.4 1.4 bitcast_add_fusion.3
  301.8 1.3 copy-done.1
  306.1 1.0 fusion.66
  307.2 1.4 bitcast_add_fusion.3
  308.6 1.3 copy-done.1
  311.1 1.0 constant_dynamic-slice_fusion.4
  312.9 1.0 fusion.66
  314.0 1.4 bitcast_add_fusion.3
  315.4 1.3 copy-done.1
  319.7 1.0 fusion.66
  320.8 1.4 bitcast_add_fusion.3
  322.2 1.3 copy-done.1
  326.5 1.0 fusion.66
  327.5 1.4 bitcast_add_fusion.3
  329.0 1.3 copy-done.1
  333.3 1.0 fusion.66
  334.3 1.4 bitcast_add_fusion.3
  335.7 1.3 copy-done.1
  340.1 1.0 fusion.66
  341.1 1.4 bitcast_add_fusion.3
  342.5 1.3 copy-done.1
  346.9 1.0 fusion.66
  347.9 1.4 bitcast_add_fusion.3
  349.3 1.3 copy-done.1
  353.6 1.0 fusion.66
  354.7 1.4 bitcast_add_fusion.3
  356.1 1.3 copy-done.1
  358.6 1.0 constant_dynamic-slice_fusion.4
  360.4 1.0 fusion.66
  361.5 1.4 bitcast_add_fusion.3
  362.9 1.3 copy-done.1
  367.2 1.0 fusion.66
  368.3 1.4 bitcast_add_fusion.3
  369.7 1.3 copy-done.1
  371.0 1.8 divide_convert_fusion
  372.8 1.4 copy.34
  (210 shorter events, 51.6 us)
Async XLA Ops:
  6.5 159.7 %all-gather.4.cloned.1.call-start = ((), (), s32[]{:S(2)}) async-start(), calls=%async_computation.1 | async-start | bytes 4456448 | tf_op jit(solution)/shard_map/all_gather | solution.py:40
  10.6 11.8 %copy-start.4 = (bf16[4096]{0:T(1024)(128)(2,1)S(1)}, bf16[4096]{0:T(1024)(128)(2,1)}, u32[]{:S(2)}) copy-start(bf16[4096]{0:T(1024)(128)(2,1)} %param.10) | copy-start | bytes 24580
  10.6 11.9 %copy-start.5 = (s32[1,256]{1,0:T(1,128)S(1)}, s32[1,256]{1,0:T(1,128)}, u32[]{:S(2)}) copy-start(s32[1,256]{1,0:T(1,128)} %param.9) | copy-start | bytes 3076
  10.6 162.5 %all-to-all-start = ((bf16[16,256,512]{2,1,0:T(8,128)(2,1)}), bf16[16,256,512]{2,1,0:T(8,128)(2,1)}, u32[]{:S(2)}, u32[]{:S(2)}) async-start(bf16[16,256,512]{2,1,0:T(8,128)(2,1)} %stack.2), calls=%async_computation | async-start | bytes 8388608 | tf_op jit(solution)/shard_map/all_to_all | solution.py:42
  22.3 198.9 %all-gather.6.cloned.1.call-start = ((), (), s32[]{:S(2)}) async-start(), calls=%async_computation.2 | async-start | bytes 4456448 | tf_op jit(solution)/shard_map/all_gather | solution.py:119
  172.9 89.6 %all-gather.8.cloned.1.call-start = ((), (), s32[]{:S(2)}) async-start(), calls=%async_computation.3 | async-start | bytes 4456448 | tf_op jit(solution)/shard_map/all_gather | solution.py:120
  173.1 5.0 %copy-start.2 = (bf16[1,256,2048]{2,1,0:T(8,128)(2,1)S(1)}, bf16[1,256,2048]{2,1,0:T(8,128)(2,1)}, u32[]{:S(2)}) copy-start(bf16[1,256,2048]{2,1,0:T(8,128)(2,1)} %param.11) | copy-start | bytes 3145732
  180.2 1.9 copy-start.3
  264.5 1.9 copy-start
  267.8 1.4 copy-start.1
  271.3 1.9 copy-start
  274.6 1.4 copy-start.1
  278.1 1.9 copy-start
  281.4 1.4 copy-start.1
  284.9 1.9 copy-start
  288.2 1.4 copy-start.1
  291.7 1.9 copy-start
  295.0 1.4 copy-start.1
  298.5 1.9 copy-start
  301.8 1.4 copy-start.1
  305.3 1.9 copy-start
  308.6 1.4 copy-start.1
  312.1 1.9 copy-start
  315.4 1.4 copy-start.1
  318.8 1.9 copy-start
  322.1 1.4 copy-start.1
  325.6 1.9 copy-start
  328.9 1.4 copy-start.1
  332.4 1.9 copy-start
  335.7 1.4 copy-start.1
  339.2 1.9 copy-start
  342.5 1.4 copy-start.1
  346.0 1.9 copy-start
  349.3 1.4 copy-start.1
  352.8 1.9 copy-start
  356.1 1.4 copy-start.1
  359.6 1.9 copy-start
  362.9 1.4 copy-start.1
  366.4 1.9 copy-start
  369.7 1.4 copy-start.1
Sparse Core Ops, SparseCore 0:
  9.9 156.2 all-gather.3
  173.0 48.2 all-gather.5
  223.1 39.2 all-gather.7
